TPU v7x, 256 devices: a whole 4x4x8 slice. The times are simulated.
256 devices in a mesh: head: 8 (over y, core), ctx: 32 (over z, x).
Axes of the slice: x: 4, y: 4, z: 8, core: 2. Of those that a mesh axis runs over, the one named last changes fastest.
Arguments:
- query_matrix: bfloat16 [32768, 4096], P(('ctx', 'head')), may hold values from -6 to 6
- key_matrix: bfloat16 [32768, 2048], P(('ctx', 'head')), may hold values from -6 to 6
- value_matrix: bfloat16 [32768, 2048], P(('ctx', 'head')), may hold values from -6 to 6
- documents: int32 [32768], replicated, may hold values from 0 to 46, as said below
- readers: int32 [32, 4], replicated, may hold values from 0 to 1, as said below
Outputs:
- attended: bfloat16 [32768, 4096], P(('ctx', 'head'))
Inputs may be any that keep to these rules, and one draw needn't show every extreme that they name: `documents`: starts at 0 and never falls from one token to the next; it rises by one exactly twice inside every key block other than key blocks 0 to 3 and 12 to 16, and nowhere else. `readers`: every entry of column 0 is 1. Row 0 and rows 12 to 16 are all 1.
All inputs are finite; a program needn't handle non-finite values.
Results may differ from a plain program's by a relative error of at most 0.0038.
Values may be sent and summed in bfloat16 or wider, within the bound.
A program may use at most 192 MiB of HBM per device.

v0:
```python
import jax
import jax.numpy as jnp
from jax import lax
from jax.sharding import PartitionSpec as P

QUERY_HEADS = 32
KEY_VALUE_HEADS = 16
HEAD_WIDTH = 128
score_scale = 168.0 ** (-0.5)
neg_large = -1e30


def passed_along(value, axis, steps):
    count = lax.axis_size(axis)
    leading, last = (max(0, -steps), min(count, count - steps))
    return lax.ppermute(value, axis, [(source, source + steps) for source in range(leading, last)])


def attend_block(running, grouped, block, query_docs, query_pos, key_docs, key_pos, allowed):
    maxima, totals, accumulated = running
    heads_local = block.shape[1] // (2 * HEAD_WIDTH)
    key_part = block[:, : heads_local * HEAD_WIDTH].reshape(block.shape[0], heads_local, HEAD_WIDTH)
    value_part = block[:, heads_local * HEAD_WIDTH :].reshape(
        block.shape[0], heads_local, HEAD_WIDTH
    )
    scores = (
        jnp.einsum("qgmd,kgd->qgmk", grouped, key_part, preferred_element_type=jnp.float32)
        * score_scale
    )
    visible = (
        (query_docs[:, None] == key_docs[None, :])
        & (key_pos[None, :] <= query_pos[:, None])
        & allowed
    )
    visible = visible[:, None, None, :]
    scores = jnp.where(visible, scores, neg_large)
    new_max = jnp.maximum(maxima, jnp.max(scores, axis=3))
    weights = jnp.where(visible, jnp.exp(scores - new_max[..., None]), 0.0)
    rescale = jnp.exp(maxima - new_max)
    totals = totals * rescale + jnp.sum(weights, axis=3)
    product = jnp.einsum(
        "qgmk,kgd->qgmd",
        weights.astype(jnp.bfloat16),
        value_part,
        preferred_element_type=jnp.float32,
    )
    accumulated = accumulated * rescale[..., None] + product
    return (new_max, totals, accumulated)


def per_device(query_matrix, key_matrix, value_matrix, documents, readers):
    query_local, key_local, value_local = (
        lax.all_to_all(query_matrix, "head", split_axis=1, concat_axis=0, tiled=True),
        lax.all_to_all(key_matrix, "head", split_axis=1, concat_axis=0, tiled=True),
        lax.all_to_all(value_matrix, "head", split_axis=1, concat_axis=0, tiled=True),
    )
    rows_per_block = query_local.shape[0]
    heads_local = key_local.shape[1] // HEAD_WIDTH
    query_group_width = QUERY_HEADS // KEY_VALUE_HEADS
    window = readers.shape[1]
    shard_index = lax.axis_index("ctx")
    stacked = jnp.concatenate([key_local, value_local], axis=1)
    block_list = [stacked] + [
        passed_along(stacked, "ctx", distance) for distance in range(1, window)
    ]
    query_start = shard_index * rows_per_block
    row_iota = jnp.arange(rows_per_block, dtype=jnp.int32)
    query_pos = query_start + row_iota
    query_docs = lax.dynamic_slice_in_dim(documents, query_start, rows_per_block)
    grouped = query_local.reshape(rows_per_block, heads_local, query_group_width, HEAD_WIDTH)
    running = (
        jnp.full((rows_per_block, heads_local, query_group_width), neg_large, jnp.float32),
        jnp.zeros((rows_per_block, heads_local, query_group_width), jnp.float32),
        jnp.zeros((rows_per_block, heads_local, query_group_width, HEAD_WIDTH), jnp.float32),
    )
    for distance in range(window):
        owner_block = shard_index - distance
        safe_owner = jnp.maximum(owner_block, 0)
        key_pos = owner_block * rows_per_block + row_iota
        key_docs = lax.dynamic_slice_in_dim(documents, safe_owner * rows_per_block, rows_per_block)
        allowed = (owner_block >= 0) & (readers[safe_owner, distance] > 0)
        running = attend_block(
            running,
            grouped,
            block_list[distance],
            query_docs,
            query_pos,
            key_docs,
            key_pos,
            allowed,
        )
    maxima, totals, accumulated = running
    outputs = (
        (accumulated / totals[..., None])
        .astype(jnp.bfloat16)
        .reshape(rows_per_block, heads_local * query_group_width * HEAD_WIDTH)
    )
    return lax.all_to_all(outputs, "head", split_axis=0, concat_axis=1, tiled=True)


def solution(mesh):
    placed = (
        P(("ctx", "head"), None),
        P(("ctx", "head"), None),
        P(("ctx", "head"), None),
        P(),
        P(),
    )
    return jax.shard_map(
        per_device, mesh=mesh, in_specs=placed, out_specs=P(("ctx", "head"), None), check_vma=False
    )
```

profile of v0, /device:TPU:128, one launch (start us, length us, event | category | flops | bytes accessed | tf_op | source)
XLA Modules:
  0.0 217.6 jit_solution(4050076900092081925)
XLA Ops:
  0.0 2.0 copy.57
  2.0 4.5 %all-to-all-start = ((bf16[128,8,256]{0,2,1:T(8,128)(2,1)}), bf16[128,8,256]{0,2,1:T(8,128)(2,1)S(1)}, u32[]{:S(2)}, u32[]{:S(2)}) async-start(bf16[128,8,256]{0,2,1:T(8,128)(2,1)} %bitcast.1), calls=%async_computation | async-start | bytes 1048576 | tf_op jit(solution)/shard_map/all_to_all | solution.py:54
  6.5 1.5 constant_dynamic-slice_fusion.3
  10.5 2.0 copy.63
  12.5 2.3 %copy.59 = bf16[128,4096]{0,1:T(8,128)(2,1)} copy(bf16[128,4096]{1,0:T(8,128)(2,1)} %param.5) | data formatting | bytes 2097152 | tf_op args[0]
  14.8 2.0 all-to-all-done
  16.8 3.5 %all-to-all-start.2 = ((bf16[128,8,256]{0,2,1:T(8,128)(2,1)}), bf16[128,8,256]{0,2,1:T(8,128)(2,1)S(1)}, u32[]{:S(2)}, u32[]{:S(2)}) async-start(bf16[128,8,256]{0,2,1:T(8,128)(2,1)} %bitcast.7), calls=%async_computation.2 | async-start | bytes 1048576 | tf_op jit(solution)/shard_map/all_to_all | solution.py:55
  20.3 0.8 fusion.52
  21.1 0.9 bitcast_dynamic-update-slice_fusion.1
  22.0 8.6 %all-to-all-done.2 = bf16[128,8,256]{0,2,1:T(8,128)(2,1)S(1)} async-done(((bf16[128,8,256]{0,2,1:T(8,128)(2,1)}), bf16[128,8,256]{0,2,1:T(8,128)(2,1)S(1)}, u32[]{:S(2)}, u32[]{:S(2)}) %all-to-all-start.2) | async-done | bytes 524320 | tf_op jit(solution)/shard_map/all_to_all | solution.py:55
  30.6 4.2 %all-to-all-start.1 = ((bf16[128,8,512]{0,2,1:T(8,128)(2,1)}), bf16[128,8,512]{0,2,1:T(8,128)(2,1)}, u32[]{:S(2)}, u32[]{:S(2)}) async-start(bf16[128,8,512]{0,2,1:T(8,128)(2,1)} %bitcast.4), calls=%async_computation.1 | async-start | bytes 2097152 | tf_op jit(solution)/shard_map/all_to_all | solution.py:53
  34.8 0.9 bitcast_dynamic-update-slice_fusion
  35.7 4.9 %collective-permute-start.1 = (bf16[1024,512]{0,1:T(8,128)(2,1)}, bf16[1024,512]{0,1:T(8,128)(2,1)}, u32[]{:S(2)}, u32[]{:S(2)}) collective-permute-start(bf16[1024,512]{0,1:T(8,128)(2,1)} %bitcast_dynamic-update-slice_fusion), channel_id=1, source_target_pairs={{0,2},{1,3},{2,4},{3,5},{4,6},{5,7},{6,8},{7,9},{8,10},{9,11},{10,... | collective-permute-start | bytes 3145736 | tf_op jit(solution)/shard_map/ppermute | solution.py:16
  40.6 5.4 %and_and_fusion.3 = (pred[1024,1024]{0,1:T(8,128)(4,1)}, pred[1024,1024]{0,1:T(8,128)(4,1)S(1)}, pred[1024,1024]{0,1:T(8,128)(4,1)S(1)}, pred[1024,1024]{0,1:T(8,128)(4,1)}) fusion(s32[1024]{0:T(1024)S(1)} %iota_add_fusion.3, s32[1024]{0:T(1024)S(1)} %get-tuple-element.20, s32[1024]{0:T(1024)S(1)} %get-tuple-element.18, pred[]{:T(512)S(6)} %and.82, ...), kind=kLoop, calls=%fused_computation.31 | loop fusion | flops 16777216 | bytes 4231172 | tf_op jit(solution)/shard_map/and | solution.py:31
  46.0 3.5 %collective-permute-start.2 = (bf16[1024,512]{0,1:T(8,128)(2,1)}, bf16[1024,512]{0,1:T(8,128)(2,1)}, u32[]{:S(2)}, u32[]{:S(2)}) collective-permute-start(bf16[1024,512]{0,1:T(8,128)(2,1)} %bitcast_dynamic-update-slice_fusion), channel_id=1, source_target_pairs={{0,3},{1,4},{2,5},{3,6},{4,7},{5,8},{6,9},{7,10},{8,11},{9,12},{10... | collective-permute-start | bytes 3145736 | tf_op jit(solution)/shard_map/ppermute | solution.py:16
  49.5 2.8 %collective-permute-start = (bf16[1024,512]{0,1:T(8,128)(2,1)}, bf16[1024,512]{0,1:T(8,128)(2,1)}, u32[]{:S(2)}, u32[]{:S(2)}) collective-permute-start(bf16[1024,512]{0,1:T(8,128)(2,1)} %bitcast_dynamic-update-slice_fusion), channel_id=1, source_target_pairs={{0,1},{1,2},{2,3},{3,4},{4,5},{5,6},{6,7},{7,8},{8,9},{9,10},{10,1... | collective-permute-start | bytes 3145736 | tf_op jit(solution)/shard_map/ppermute | solution.py:16
  52.3 1.1 copy.58
  53.4 2.1 reshape.334
  55.5 0.3 copy.64
  55.9 1.0 reshape.336
  56.9 0.0 all-to-all-done.1
  56.9 1.9 copy.60
  58.8 1.3 reshape.335
  60.1 10.8 %fusion = (f32[1024,2,2]{0,2,1:T(2,128)S(1)}, f32[2,1024,1024,2]{2,1,3,0:T(8,128)}) fusion(pred[1024,1024]{0,1:T(8,128)(4,1)} %get-tuple-element.25, bf16[1024,2,2,128]{0,3,2,1:T(8,128)(2,1)} %reshape.335, bf16[1024,2,128]{0,2,1:T(8,128)(2,1)} %reshape.334), kind=kOutput, calls=%fused_computation.8 | convolution fusion | flops 1086320640 | bytes 19415040 | tf_op jit(solution)/shard_map/qgmd,kgd->qgmk/dot_general | solution.py:27
  70.8 0.0 collective-permute-done.1
  70.8 2.1 fusion.51
  72.9 0.0 copy-done.1
  72.9 7.5 %fusion.2 = (f32[1024,2,2]{0,2,1:T(2,128)S(1)}, f32[2,1024,1024,2]{2,1,3,0:T(8,128)}) fusion(pred[1024,1024]{0,1:T(8,128)(4,1)S(1)} %get-tuple-element.26, bf16[1024,2,128,1]{0,2,3,1:T(8,128)(2,1)S(1)} %bitcast.168, bf16[1024,2,2,128]{0,3,2,1:T(8,128)(2,1)S(1)} %copy-done.1), kind=kOutput, calls=%fused_computation.10 | convolution fusion | flops 1086320640 | bytes 19415040 | tf_op jit(solution)/shard_map/qgmd,kgd->qgmk/dot_general | solution.py:27
  80.5 0.0 collective-permute-done.2
  80.5 2.1 fusion.49
  82.6 7.5 %fusion.3 = (f32[1024,2,2]{0,2,1:T(2,128)S(1)}, f32[2,1024,1024,2]{2,1,3,0:T(8,128)}) fusion(pred[1024,1024]{0,1:T(8,128)(4,1)S(1)} %get-tuple-element.27, bf16[1024,2,128,1]{0,2,3,1:T(8,128)(2,1)S(1)} %bitcast.169, bf16[1024,2,2,128]{0,3,2,1:T(8,128)(2,1)S(1)} %copy-done.1), kind=kOutput, calls=%fused_computation.11 | convolution fusion | flops 1086320640 | bytes 19415040 | tf_op jit(solution)/shard_map/qgmd,kgd->qgmk/dot_general | solution.py:27
  90.2 22.5 %collective-permute-done = bf16[1024,512]{0,1:T(8,128)(2,1)} collective-permute-done((bf16[1024,512]{0,1:T(8,128)(2,1)}, bf16[1024,512]{0,1:T(8,128)(2,1)}, u32[]{:S(2)}, u32[]{:S(2)}) %collective-permute-start) | collective-permute-done | bytes 1048608 | tf_op jit(solution)/shard_map/ppermute | solution.py:16
  112.7 2.1 fusion.50
  114.7 0.0 copy-done
  114.7 7.6 %fusion.1 = (f32[1024,2,2]{0,2,1:T(2,128)S(1)}, f32[2,1024,1024,2]{2,1,3,0:T(8,128)}) fusion(pred[1024,1024]{0,1:T(8,128)(4,1)S(1)} %copy-done, bf16[1024,2,128,1]{0,2,3,1:T(8,128)(2,1)S(1)} %bitcast.167, bf16[1024,2,2,128]{0,3,2,1:T(8,128)(2,1)S(1)} %copy-done.1), kind=kOutput, calls=%fused_computation.9 | convolution fusion | flops 1086320640 | bytes 19415040 | tf_op jit(solution)/shard_map/qgmd,kgd->qgmk/dot_general | solution.py:27
  122.3 13.5 %fusion.18 = f32[2,1024,2,128]{3,1,2,0:T(8,128)} fusion(f32[2,1024,1024,2]{2,1,3,0:T(8,128)} %get-tuple-element.40, f32[1024,2,2]{0,2,1:T(2,128)S(1)} %get-tuple-element.24, pred[1024,1024]{0,1:T(8,128)(4,1)} %get-tuple-element.25, bf16[1024,2,128]{0,2,1:T(8,128)(2,1)} %reshape.336), kind=kOutput, calls=%fused_computation.23 | convolution fusion | flops 1094713344 | bytes 20463616 | tf_op jit(solution)/shard_map/qgmk,kgd->qgmd/dot_general | solution.py:41
  135.9 14.0 %fusion.4 = (f32[1024,2,2]{0,2,1:T(2,128)S(1)}, f32[1024,2,2]{0,2,1:T(2,128)S(1)}) fusion(f32[2,1024,1024,2]{2,1,3,0:T(8,128)} %get-tuple-element.40, f32[1024,2,2]{0,2,1:T(2,128)S(1)} %get-tuple-element.24, pred[1024,1024]{0,1:T(8,128)(4,1)} %get-tuple-element.25, f32[1024,2,2]{0,2,1:T(2,128)S(1)} %get-tuple-element.11, ...), kind=kLoop, calls=%fused_computation.12 | loop fusion | flops 41934848 | bytes 35717120 | tf_op jit(solution)/shard_map/reduce_sum | solution.py:40
  149.9 10.7 %fusion.16 = f32[2,128,1024,2]{1,2,3,0:T(8,128)} fusion(bf16[1024,2,128,1]{0,2,3,1:T(8,128)(2,1)S(1)} %bitcast.166, f32[2,1024,1024,2]{2,1,3,0:T(8,128)} %get-tuple-element.38, f32[1024,2,2]{0,2,1:T(2,128)S(1)} %get-tuple-element.11, pred[1024,1024]{0,1:T(8,128)(4,1)S(1)} %copy-done), kind=kOutput, calls=%fused_computation.22 | convolution fusion | flops 1094713344 | bytes 20463616 | tf_op jit(solution)/shard_map/qgmk,kgd->qgmd/dot_general | solution.py:41
  160.6 11.0 %fusion.14 = f32[2,128,1024,2]{1,2,3,0:T(8,128)} fusion(bf16[1024,2,128,1]{0,2,3,1:T(8,128)(2,1)S(1)} %bitcast.165, f32[2,1024,1024,2]{2,1,3,0:T(8,128)} %get-tuple-element.36, f32[1024,2,2]{0,2,1:T(2,128)S(1)} %get-tuple-element.10, pred[1024,1024]{0,1:T(8,128)(4,1)S(1)} %get-tuple-element.26), kind=kOutput, calls=%fused_computation.21 | convolution fusion | flops 1094713344 | bytes 20463616 | tf_op jit(solution)/shard_map/qgmk,kgd->qgmd/dot_general | solution.py:41
  171.6 14.7 %fusion.8 = (f32[1024,2,2]{0,2,1:T(2,128)S(1)}, f32[1024,2,2]{0,2,1:T(2,128)S(1)}) fusion(f32[2,1024,1024,2]{2,1,3,0:T(8,128)} %get-tuple-element.36, f32[1024,2,2]{0,2,1:T(2,128)S(1)} %get-tuple-element.10, pred[1024,1024]{0,1:T(8,128)(4,1)S(1)} %get-tuple-element.26, f32[1024,2,2]{0,2,1:T(2,128)S(1)} %get-tuple-element.9, ...), kind=kLoop, calls=%fused_computation.16 | loop fusion | flops 41934848 | bytes 35717120 | tf_op jit(solution)/shard_map/reduce_sum | solution.py:40
  186.3 0.1 multiply_add_fusion
  186.5 0.3 copy-done.7
  186.8 8.3 %fusion.25 = bf16[1024,2,2,128]{3,0,2,1:T(8,128)(2,1)S(1)} fusion(f32[2,128,1024,2]{1,2,3,0:T(8,128)S(1)} %copy-done.7, f32[2,128,1024,2]{1,2,3,0:T(8,128)S(1)} %copy-done.6, f32[2,1024,2,128]{3,1,2,0:T(8,128)S(1)} %copy-done.5, bf16[1024,2,128,1]{0,2,3,1:T(8,128)(2,1)S(1)} %bitcast.164, f32[2,1024,1024,2]{2,1,3,0:T(8,128)S(1)} %bitcast.158, ...), kind=kOutput, calls=%fused_computation.34 | convolution fusion | flops 1099431936 | bytes 25788416 | tf_op jit(solution)/shard_map/qgmk,kgd->qgmd/dot_general | solution.py:41
  195.1 0.5 copy.81
  195.6 0.3 copy.115
  195.9 0.1 copy.82
  196.1 20.2 %all_to_all.73 = bf16[8,128,512]{1,2,0:T(8,128)(2,1)S(1)} all-to-all(bf16[8,128,512]{1,2,0:T(8,128)(2,1)S(1)} %copy.82), channel_id=1, replica_groups=mesh['head'=8,'ctx'=32] {'head'}, dimensions={0} | all-to-all | bytes 2097152 | tf_op jit(solution)/shard_map/all_to_all | solution.py:98
  216.3 1.3 copy.83
  (27 shorter events, 0.1 us)
Async XLA Ops:
  2.0 14.8 %all-to-all-start = ((bf16[128,8,256]{0,2,1:T(8,128)(2,1)}), bf16[128,8,256]{0,2,1:T(8,128)(2,1)S(1)}, u32[]{:S(2)}, u32[]{:S(2)}) async-start(bf16[128,8,256]{0,2,1:T(8,128)(2,1)} %bitcast.1), calls=%async_computation | async-start | bytes 1048576 | tf_op jit(solution)/shard_map/all_to_all | solution.py:54
  16.8 13.7 %all-to-all-start.2 = ((bf16[128,8,256]{0,2,1:T(8,128)(2,1)}), bf16[128,8,256]{0,2,1:T(8,128)(2,1)S(1)}, u32[]{:S(2)}, u32[]{:S(2)}) async-start(bf16[128,8,256]{0,2,1:T(8,128)(2,1)} %bitcast.7), calls=%async_computation.2 | async-start | bytes 1048576 | tf_op jit(solution)/shard_map/all_to_all | solution.py:55
  30.6 26.3 %all-to-all-start.1 = ((bf16[128,8,512]{0,2,1:T(8,128)(2,1)}), bf16[128,8,512]{0,2,1:T(8,128)(2,1)}, u32[]{:S(2)}, u32[]{:S(2)}) async-start(bf16[128,8,512]{0,2,1:T(8,128)(2,1)} %bitcast.4), calls=%async_computation.1 | async-start | bytes 2097152 | tf_op jit(solution)/shard_map/all_to_all | solution.py:53
  35.7 35.1 %collective-permute-start.1 = (bf16[1024,512]{0,1:T(8,128)(2,1)}, bf16[1024,512]{0,1:T(8,128)(2,1)}, u32[]{:S(2)}, u32[]{:S(2)}) collective-permute-start(bf16[1024,512]{0,1:T(8,128)(2,1)} %bitcast_dynamic-update-slice_fusion), channel_id=1, source_target_pairs={{0,2},{1,3},{2,4},{3,5},{4,6},{5,7},{6,8},{7,9},{8,10},{9,11},{10,... | collective-permute-start | bytes 3145736 | tf_op jit(solution)/shard_map/ppermute | solution.py:16
  46.0 34.5 %collective-permute-start.2 = (bf16[1024,512]{0,1:T(8,128)(2,1)}, bf16[1024,512]{0,1:T(8,128)(2,1)}, u32[]{:S(2)}, u32[]{:S(2)}) collective-permute-start(bf16[1024,512]{0,1:T(8,128)(2,1)} %bitcast_dynamic-update-slice_fusion), channel_id=1, source_target_pairs={{0,3},{1,4},{2,5},{3,6},{4,7},{5,8},{6,9},{7,10},{8,11},{9,12},{10... | collective-permute-start | bytes 3145736 | tf_op jit(solution)/shard_map/ppermute | solution.py:16
  49.5 63.2 %collective-permute-start = (bf16[1024,512]{0,1:T(8,128)(2,1)}, bf16[1024,512]{0,1:T(8,128)(2,1)}, u32[]{:S(2)}, u32[]{:S(2)}) collective-permute-start(bf16[1024,512]{0,1:T(8,128)(2,1)} %bitcast_dynamic-update-slice_fusion), channel_id=1, source_target_pairs={{0,1},{1,2},{2,3},{3,4},{4,5},{5,6},{6,7},{7,8},{8,9},{9,10},{10,1... | collective-permute-start | bytes 3145736 | tf_op jit(solution)/shard_map/ppermute | solution.py:16
  60.1 12.9 %copy-start.1 = (bf16[1024,2,2,128]{0,3,2,1:T(8,128)(2,1)S(1)}, bf16[1024,2,2,128]{0,3,2,1:T(8,128)(2,1)}, u32[]{:S(2)}) copy-start(bf16[1024,2,2,128]{0,3,2,1:T(8,128)(2,1)} %reshape.335) | copy-start | bytes 3145732
  80.5 34.3 %copy-start = (pred[1024,1024]{0,1:T(8,128)(4,1)S(1)}, pred[1024,1024]{0,1:T(8,128)(4,1)}, u32[]{:S(2)}) copy-start(pred[1024,1024]{0,1:T(8,128)(4,1)} %get-tuple-element.28) | copy-start | bytes 3145732
  135.9 14.0 %copy-start.4 = (bf16[1024,256]{0,1:T(8,128)(2,1)S(1)}, bf16[1024,256]{0,1:T(8,128)(2,1)}, u32[]{:S(2)}) copy-start(bf16[1024,256]{0,1:T(8,128)(2,1)} %get-tuple-element.14) | copy-start | bytes 1572868
  149.9 10.7 %copy-start.3 = (bf16[1024,256]{0,1:T(8,128)(2,1)S(1)}, bf16[1024,256]{0,1:T(8,128)(2,1)}, u32[]{:S(2)}) copy-start(bf16[1024,256]{0,1:T(8,128)(2,1)} %get-tuple-element.17) | copy-start | bytes 1572868
  160.6 25.8 %slice-start = ((s8[16777216]{0:T(1024)(128)(4,1)}), s8[4194304]{0:T(1024)(128)(4,1)S(1)}, s32[]{:S(2)}) async-start(s8[16777216]{0:T(1024)(128)(4,1)} %bitcast.157), calls=%async_computation.4 | async-start | bytes 8388608
  160.6 25.8 %slice-start.1 = ((s8[16777216]{0:T(1024)(128)(4,1)}), s8[4194304]{0:T(1024)(128)(4,1)S(1)}, s32[]{:S(2)}) async-start(s8[16777216]{0:T(1024)(128)(4,1)} %bitcast.157), calls=%async_computation.5 | async-start | bytes 8388608
  171.6 14.8 %slice-start.2 = ((s8[16777216]{0:T(1024)(128)(4,1)}), s8[4194304]{0:T(1024)(128)(4,1)S(1)}, s32[]{:S(2)}) async-start(s8[16777216]{0:T(1024)(128)(4,1)} %bitcast.157), calls=%async_computation.6 | async-start | bytes 8388608
  171.6 14.8 %slice-start.3 = ((s8[16777216]{0:T(1024)(128)(4,1)}), s8[4194304]{0:T(1024)(128)(4,1)S(1)}, s32[]{:S(2)}) async-start(s8[16777216]{0:T(1024)(128)(4,1)} %bitcast.157), calls=%async_computation.7 | async-start | bytes 8388608
  171.6 14.8 %copy-start.2 = (bf16[1024,256]{0,1:T(8,128)(2,1)S(1)}, bf16[1024,256]{0,1:T(8,128)(2,1)}, u32[]{:S(2)}) copy-start(bf16[1024,256]{0,1:T(8,128)(2,1)} %get-tuple-element.12) | copy-start | bytes 1572868
  171.6 14.8 %copy-start.5 = (f32[2,1024,2,128]{3,1,2,0:T(8,128)S(1)}, f32[2,1024,2,128]{3,1,2,0:T(8,128)}, u32[]{:S(2)}) copy-start(f32[2,1024,2,128]{3,1,2,0:T(8,128)} %fusion.18) | copy-start | bytes 6291460
  171.6 14.8 %copy-start.6 = (f32[2,128,1024,2]{1,2,3,0:T(8,128)S(1)}, f32[2,128,1024,2]{1,2,3,0:T(8,128)}, u32[]{:S(2)}) copy-start(f32[2,128,1024,2]{1,2,3,0:T(8,128)} %fusion.16) | copy-start | bytes 6291460
  171.6 15.1 %copy-start.7 = (f32[2,128,1024,2]{1,2,3,0:T(8,128)S(1)}, f32[2,128,1024,2]{1,2,3,0:T(8,128)}, u32[]{:S(2)}) copy-start(f32[2,128,1024,2]{1,2,3,0:T(8,128)} %fusion.14) | copy-start | bytes 6291460
where the time goes:
time: 218 us
  matrix products  77 us (35%)
  other arithmetic  34.2 us (16%)
  waiting for transfers between devices  33.1 us (15%)
  local copies, waits for them, and re-layouts  27 us (12%)
  starting transfers between devices  23.4 us (11%)
  blocking collectives  20.2 us (9%)
  between operations  2.73 us (1%)
    dot_general x4, matrix products, attend_block(): jnp.einsum('qgmk,kgd->qgmd', weights.astype(jnp.bfloat16), value_part, pr...  43.6 us
    dot_general x4, matrix products, attend_block(): jnp.einsum('qgmd,kgd->qgmk', grouped, key_part, preferred_element_type=jn...  33.4 us
    reduce_sum x2, other arithmetic, attend_block(): totals = totals * rescale + jnp.sum(weights, axis=3)  28.7 us
    ppermute x3, waiting for transfers between devices, passed_along(): lax.ppermute(value, axis, [(source, source + steps) for source in range(l...  22.5 us
    all_to_all x1, blocking collectives, per_device(): lax.all_to_all(outputs, 'head', split_axis=0, concat_axis=1, tiled=True)  20.2 us
    ppermute x3, starting transfers between devices, passed_along(): lax.ppermute(value, axis, [(source, source + steps) for source in range(l...  11.2 us
    all_to_all x1, waiting for transfers between devices, per_device(): lax.all_to_all(value_matrix, 'head', split_axis=1, concat_axis=0, tiled=T...  8.57 us
    unnamed x29, local copies, waits for them, and re-layouts  7.82 us
  transfers between devices with their start and end apart: 6, of which 3 were waited for; matrix products, arithmetic and copies ran while one was open for 24% of the time, Pallas kernels for 0%

commit v1 on v0

--- a/solution.py
+++ b/solution.py
@@ -1,3 +1,4 @@
+import functools
 import jax
 import jax.numpy as jnp
 from jax import lax
@@ -8,6 +9,18 @@
 HEAD_WIDTH = 128
 score_scale = 168.0 ** (-0.5)
 neg_large = -1e30
+
+
+def search_the_sheets(xin, axis_tag):
+    return jnp.concatenate(
+        lax.all_to_all(
+            jnp.stack(jnp.split(xin, lax.axis_size(axis_tag), axis=0), axis=0), axis_tag, 0, 0
+        ),
+        axis=1,
+    )
+
+
+_rest_pairs_all = functools.partial(search_the_sheets, axis_tag="head")
 
 
 def passed_along(value, axis, steps):
@@ -95,7 +108,7 @@
         .astype(jnp.bfloat16)
         .reshape(rows_per_block, heads_local * query_group_width * HEAD_WIDTH)
     )
-    return lax.all_to_all(outputs, "head", split_axis=0, concat_axis=1, tiled=True)
+    return _rest_pairs_all(outputs)
 
 
 def solution(mesh):

time: 218 us -> 207 us (0.950)
  matrix products: 77 us -> 66.6 us
  other arithmetic: 34.2 us -> 30.2 us
  waiting for transfers between devices: 33.1 us -> 36.6 us
    dot_general x4, matrix products: 43.6 us -> 37.4 us  [attend_block(): jnp.einsum('qgmk,kgd->qgmd', weights.astype(jnp.bfloat16), value_part, pr...]
    dot_general x4, matrix products: 33.4 us -> 29.3 us  [attend_block(): jnp.einsum('qgmd,kgd->qgmk', grouped, key_part, preferred_element_type=jn...]
    reduce_sum x2, other arithmetic: 28.7 us -> 24.6 us  [attend_block(): totals = totals * rescale + jnp.sum(weights, axis=3)]
    ppermute x3, waiting for transfers between devices: 22.5 us -> 26.1 us  [passed_along(): lax.ppermute(value, axis, [(source, source + steps) for source in range(l...]
    unnamed x29 -> x21, local copies, waits for them, and re-layouts: 7.82 us -> 7.37 us
  transfers between devices with their start and end apart: 6 -> 6, of which waited for: 3 -> 3; matrix products, arithmetic and copies ran while one was open for 24% -> 23% of each run, Pallas kernels for 0% -> 0%
where the time goes in v1:
time: 207 us; the launch traced here: 206 us
  matrix products  66.6 us (32%)
  waiting for transfers between devices  36.6 us (18%)
  other arithmetic  30.2 us (15%)
  local copies, waits for them, and re-layouts  26.6 us (13%)
  starting transfers between devices  23.4 us (11%)
  blocking collectives  20.2 us (10%)
  between operations  2.74 us (1%)
    dot_general x4, matrix products, attend_block(): jnp.einsum('qgmk,kgd->qgmd', weights.astype(jnp.bfloat16), value_part, pr...  37.4 us
    dot_general x4, matrix products, attend_block(): jnp.einsum('qgmd,kgd->qgmk', grouped, key_part, preferred_element_type=jn...  29.3 us
    ppermute x3, waiting for transfers between devices, passed_along(): lax.ppermute(value, axis, [(source, source + steps) for source in range(l...  26.1 us
    reduce_sum x2, other arithmetic, attend_block(): totals = totals * rescale + jnp.sum(weights, axis=3)  24.6 us
    all_to_all x1, blocking collectives, search_the_sheets(): lax.all_to_all(jnp.stack(jnp.split(xin, lax.axis_size(axis_tag), axis=0),...  20.2 us
    ppermute x3, starting transfers between devices, passed_along(): lax.ppermute(value, axis, [(source, source + steps) for source in range(l...  11.2 us
    all_to_all x1, waiting for transfers between devices, per_device(): lax.all_to_all(value_matrix, 'head', split_axis=1, concat_axis=0, tiled=T...  8.57 us
    unnamed x21, local copies, waits for them, and re-layouts  7.37 us
  transfers between devices with their start and end apart: 6, of which 3 were waited for; matrix products, arithmetic and copies ran while one was open for 23% of the time, Pallas kernels for 0%

profile of v1, /device:TPU:128, one launch (start us, length us, event | category | flops | bytes accessed | tf_op | source)
XLA Modules:
  0.0 206.4 jit_solution(7923619695191297150)
XLA Ops:
  0.0 2.0 copy.29
  2.0 4.5 %all-to-all-start = ((bf16[128,8,256]{0,2,1:T(8,128)(2,1)}), bf16[128,8,256]{0,2,1:T(8,128)(2,1)S(1)}, u32[]{:S(2)}, u32[]{:S(2)}) async-start(bf16[128,8,256]{0,2,1:T(8,128)(2,1)} %bitcast.1), calls=%async_computation | async-start | bytes 1048576 | tf_op jit(solution)/shard_map/all_to_all | solution.py:67
  6.5 1.5 constant_dynamic-slice_fusion.3
  10.5 2.0 copy.35
  12.5 2.3 %copy.31 = bf16[128,4096]{0,1:T(8,128)(2,1)} copy(bf16[128,4096]{1,0:T(8,128)(2,1)} %param.5) | data formatting | bytes 2097152 | tf_op args[0]
  14.8 2.0 all-to-all-done
  16.8 3.5 %all-to-all-start.2 = ((bf16[128,8,256]{0,2,1:T(8,128)(2,1)}), bf16[128,8,256]{0,2,1:T(8,128)(2,1)S(1)}, u32[]{:S(2)}, u32[]{:S(2)}) async-start(bf16[128,8,256]{0,2,1:T(8,128)(2,1)} %bitcast.7), calls=%async_computation.2 | async-start | bytes 1048576 | tf_op jit(solution)/shard_map/all_to_all | solution.py:68
  20.3 0.8 fusion.53
  21.1 0.9 bitcast_dynamic-update-slice_fusion.1
  22.0 8.6 %all-to-all-done.2 = bf16[128,8,256]{0,2,1:T(8,128)(2,1)S(1)} async-done(((bf16[128,8,256]{0,2,1:T(8,128)(2,1)}), bf16[128,8,256]{0,2,1:T(8,128)(2,1)S(1)}, u32[]{:S(2)}, u32[]{:S(2)}) %all-to-all-start.2) | async-done | bytes 524320 | tf_op jit(solution)/shard_map/all_to_all | solution.py:68
  30.6 4.2 %all-to-all-start.1 = ((bf16[128,8,512]{0,2,1:T(8,128)(2,1)}), bf16[128,8,512]{0,2,1:T(8,128)(2,1)}, u32[]{:S(2)}, u32[]{:S(2)}) async-start(bf16[128,8,512]{0,2,1:T(8,128)(2,1)} %bitcast.4), calls=%async_computation.1 | async-start | bytes 2097152 | tf_op jit(solution)/shard_map/all_to_all | solution.py:66
  34.8 0.9 bitcast_dynamic-update-slice_fusion
  35.7 4.9 %collective-permute-start.1 = (bf16[1024,512]{0,1:T(8,128)(2,1)}, bf16[1024,512]{0,1:T(8,128)(2,1)}, u32[]{:S(2)}, u32[]{:S(2)}) collective-permute-start(bf16[1024,512]{0,1:T(8,128)(2,1)} %bitcast_dynamic-update-slice_fusion), channel_id=1, source_target_pairs={{0,2},{1,3},{2,4},{3,5},{4,6},{5,7},{6,8},{7,9},{8,10},{9,11},{10,... | collective-permute-start | bytes 3145736 | tf_op jit(solution)/shard_map/ppermute | solution.py:29
  40.6 5.4 %and_and_fusion.3 = (pred[1024,1024]{0,1:T(8,128)(4,1)}, pred[1024,1024]{0,1:T(8,128)(4,1)S(1)}, pred[1024,1024]{0,1:T(8,128)(4,1)S(1)}, pred[1024,1024]{0,1:T(8,128)(4,1)}) fusion(s32[1024]{0:T(1024)S(1)} %iota_add_fusion.3, s32[1024]{0:T(1024)S(1)} %get-tuple-element.28, s32[1024]{0:T(1024)S(1)} %get-tuple-element.26, pred[]{:T(512)S(6)} %and.82, ...), kind=kLoop, calls=%fused_computation.31 | loop fusion | flops 16777216 | bytes 4231172 | tf_op jit(solution)/shard_map/and | solution.py:44
  46.1 3.5 %collective-permute-start.2 = (bf16[1024,512]{0,1:T(8,128)(2,1)}, bf16[1024,512]{0,1:T(8,128)(2,1)}, u32[]{:S(2)}, u32[]{:S(2)}) collective-permute-start(bf16[1024,512]{0,1:T(8,128)(2,1)} %bitcast_dynamic-update-slice_fusion), channel_id=1, source_target_pairs={{0,3},{1,4},{2,5},{3,6},{4,7},{5,8},{6,9},{7,10},{8,11},{9,12},{10... | collective-permute-start | bytes 3145736 | tf_op jit(solution)/shard_map/ppermute | solution.py:29
  49.6 2.8 %collective-permute-start = (bf16[1024,512]{0,1:T(8,128)(2,1)}, bf16[1024,512]{0,1:T(8,128)(2,1)}, u32[]{:S(2)}, u32[]{:S(2)}) collective-permute-start(bf16[1024,512]{0,1:T(8,128)(2,1)} %bitcast_dynamic-update-slice_fusion), channel_id=1, source_target_pairs={{0,1},{1,2},{2,3},{3,4},{4,5},{5,6},{6,7},{7,8},{8,9},{9,10},{10,1... | collective-permute-start | bytes 3145736 | tf_op jit(solution)/shard_map/ppermute | solution.py:29
  52.4 1.2 copy.30
  53.5 2.1 %reshape.352 = bf16[1024,2,128]{0,2,1:T(8,128)(2,1)} reshape(bf16[8,128,256]{1,0,2:T(8,128)(2,1)} %copy.30) | data formatting | bytes 1048576 | tf_op jit(solution)/shard_map/reshape | solution.py:35
  55.6 0.3 copy.36
  55.9 0.2 reshape.364
  56.2 0.0 all-to-all-done.1
  56.2 2.9 %copy.32 = bf16[8,128,512]{1,0,2:T(8,128)(2,1)} copy(bf16[8,128,512]{1,2,0:T(8,128)(2,1)} %bitcast.5) | data formatting | bytes 2097152 | tf_op jit(solution)/shard_map/all_to_all | solution.py:66
  59.1 2.3 %reshape.353 = bf16[1024,2,2,128]{0,3,2,1:T(8,128)(2,1)} reshape(bf16[8,128,512]{1,0,2:T(8,128)(2,1)} %copy.32) | data formatting | bytes 2097152 | tf_op jit(solution)/shard_map/reshape | solution.py:83
  61.4 10.8 %fusion = (f32[1024,2,2]{0,2,1:T(2,128)S(1)}, f32[2,1024,1024,2]{2,1,3,0:T(8,128)}) fusion(pred[1024,1024]{0,1:T(8,128)(4,1)} %get-tuple-element.33, bf16[1024,2,2,128]{0,3,2,1:T(8,128)(2,1)} %reshape.353, bf16[1024,2,128]{0,2,1:T(8,128)(2,1)} %reshape.352), kind=kOutput, calls=%fused_computation.8 | convolution fusion | flops 1086320640 | bytes 19415040 | tf_op jit(solution)/shard_map/qgmd,kgd->qgmk/dot_general | solution.py:40
  72.2 0.0 collective-permute-done.1
  72.2 2.1 %fusion.52 = (bf16[1024,256]{0,1:T(8,128)(2,1)S(1)}, bf16[1024,256]{0,1:T(8,128)(2,1)}) fusion(bf16[1024,512]{0,1:T(8,128)(2,1)} %collective-permute-done.1), kind=kLoop, calls=%fused_computation.85 | loop fusion | bytes 2097152 | tf_op jit(solution)/shard_map/slice | solution.py:35
  74.3 0.0 copy-done.2
  74.3 7.6 %fusion.2 = (f32[1024,2,2]{0,2,1:T(2,128)S(1)}, f32[2,1024,1024,2]{2,1,3,0:T(8,128)}) fusion(pred[1024,1024]{0,1:T(8,128)(4,1)S(1)} %get-tuple-element.34, bf16[1024,2,128,1]{0,2,3,1:T(8,128)(2,1)S(1)} %bitcast.172, bf16[1024,2,2,128]{0,3,2,1:T(8,128)(2,1)S(1)} %copy-done.2), kind=kOutput, calls=%fused_computation.10 | convolution fusion | flops 1086320640 | bytes 19415040 | tf_op jit(solution)/shard_map/qgmd,kgd->qgmk/dot_general | solution.py:40
  81.8 0.0 collective-permute-done.2
  81.8 1.4 fusion.50
  83.2 0.0 copy-start.1
  83.2 3.4 %fusion.3 = (f32[1024,2,2]{0,2,1:T(2,128)S(1)}, f32[2,1024,1024,2]{2,1,3,0:T(8,128)S(1)}) fusion(pred[1024,1024]{0,1:T(8,128)(4,1)S(1)} %get-tuple-element.35, bf16[1024,2,128,1]{0,2,3,1:T(8,128)(2,1)S(1)} %bitcast.173, bf16[1024,2,2,128]{0,3,2,1:T(8,128)(2,1)S(1)} %copy-done.2), kind=kOutput, calls=%fused_computation.11 | convolution fusion | flops 1086320640 | bytes 19415040 | tf_op jit(solution)/shard_map/qgmd,kgd->qgmk/dot_general | solution.py:40
  86.6 26.1 %collective-permute-done = bf16[1024,512]{0,1:T(8,128)(2,1)} collective-permute-done((bf16[1024,512]{0,1:T(8,128)(2,1)}, bf16[1024,512]{0,1:T(8,128)(2,1)}, u32[]{:S(2)}, u32[]{:S(2)}) %collective-permute-start) | collective-permute-done | bytes 1048608 | tf_op jit(solution)/shard_map/ppermute | solution.py:29
  112.7 2.1 fusion.51
  114.7 0.0 copy-done
  114.7 7.5 %fusion.1 = (f32[1024,2,2]{0,2,1:T(2,128)S(1)}, f32[2,1024,1024,2]{2,1,3,0:T(8,128)}) fusion(pred[1024,1024]{0,1:T(8,128)(4,1)S(1)} %copy-done, bf16[1024,2,128,1]{0,2,3,1:T(8,128)(2,1)S(1)} %bitcast.171, bf16[1024,2,2,128]{0,3,2,1:T(8,128)(2,1)S(1)} %copy-done.2), kind=kOutput, calls=%fused_computation.9 | convolution fusion | flops 1086320640 | bytes 19415040 | tf_op jit(solution)/shard_map/qgmd,kgd->qgmk/dot_general | solution.py:40
  122.3 0.0 copy-done.1
  122.3 10.2 %fusion.18 = f32[2,1024,2,128]{1,3,2,0:T(8,128)} fusion(f32[2,1024,1024,2]{2,1,3,0:T(8,128)} %get-tuple-element.48, f32[1024,2,2]{0,2,1:T(2,128)S(1)} %get-tuple-element.32, pred[1024,1024]{0,1:T(8,128)(4,1)S(1)} %copy-done.1, bf16[1024,2,128,1]{0,2,1,3:T(8,128)(2,1)S(1)} %reshape.364), kind=kOutput, calls=%fused_computation.23 | convolution fusion | flops 1094713344 | bytes 20463616 | tf_op jit(solution)/shard_map/qgmk,kgd->qgmd/dot_general | solution.py:54
  132.6 13.7 %fusion.4 = (f32[1024,2,2]{0,2,1:T(2,128)S(1)}, f32[1024,2,2]{0,2,1:T(2,128)S(1)}) fusion(f32[2,1024,1024,2]{2,1,3,0:T(8,128)} %get-tuple-element.48, f32[1024,2,2]{0,2,1:T(2,128)S(1)} %get-tuple-element.32, pred[1024,1024]{0,1:T(8,128)(4,1)S(1)} %copy-done.1, f32[1024,2,2]{0,2,1:T(2,128)S(1)} %get-tuple-element.11, ...), kind=kLoop, calls=%fused_computation.12 | loop fusion | flops 41934848 | bytes 35717120 | tf_op jit(solution)/shard_map/reduce_sum | solution.py:53
  146.3 10.1 %fusion.16 = f32[2,128,1024,2]{2,1,3,0:T(8,128)} fusion(bf16[1024,2,128,1]{0,2,3,1:T(8,128)(2,1)S(1)} %bitcast.170, f32[2,1024,1024,2]{2,1,3,0:T(8,128)} %get-tuple-element.46, f32[1024,2,2]{0,2,1:T(2,128)S(1)} %get-tuple-element.11, pred[1024,1024]{0,1:T(8,128)(4,1)S(1)} %copy-done), kind=kOutput, calls=%fused_computation.22 | convolution fusion | flops 1094713344 | bytes 20463616 | tf_op jit(solution)/shard_map/qgmk,kgd->qgmd/dot_general | solution.py:54
  156.4 0.0 copy-done.3
  156.4 9.9 %fusion.14 = f32[2,128,1024,2]{2,1,3,0:T(8,128)} fusion(bf16[1024,2,128,1]{0,2,3,1:T(8,128)(2,1)S(1)} %bitcast.169, f32[2,1024,1024,2]{2,1,3,0:T(8,128)} %get-tuple-element.44, f32[1024,2,2]{0,2,1:T(2,128)S(1)} %get-tuple-element.10, pred[1024,1024]{0,1:T(8,128)(4,1)S(1)} %get-tuple-element.34), kind=kOutput, calls=%fused_computation.21 | convolution fusion | flops 1094713344 | bytes 20463616 | tf_op jit(solution)/shard_map/qgmk,kgd->qgmd/dot_general | solution.py:54
  166.3 10.9 %fusion.8 = (f32[1024,2,2]{0,2,1:T(2,128)S(1)}, f32[1024,2,2]{0,2,1:T(2,128)S(1)}) fusion(f32[2,1024,1024,2]{2,1,3,0:T(8,128)} %get-tuple-element.44, f32[1024,2,2]{0,2,1:T(2,128)S(1)} %get-tuple-element.10, pred[1024,1024]{0,1:T(8,128)(4,1)S(1)} %get-tuple-element.34, f32[1024,2,2]{0,2,1:T(2,128)S(1)} %get-tuple-element.9, ...), kind=kLoop, calls=%fused_computation.16 | loop fusion | flops 41934848 | bytes 35717120 | tf_op jit(solution)/shard_map/reduce_sum | solution.py:53
  177.2 0.1 multiply_add_fusion
  177.3 7.2 %fusion.25 = bf16[1024,2,2,128]{0,3,2,1:T(8,128)(2,1)S(1)} fusion(f32[2,128,1024,2]{2,1,3,0:T(8,128)} %fusion.14, f32[2,128,1024,2]{2,1,3,0:T(8,128)} %fusion.16, f32[2,1024,2,128]{1,3,2,0:T(8,128)} %fusion.18, bf16[1024,2,128,1]{0,2,3,1:T(8,128)(2,1)S(1)} %bitcast.168, f32[2,1024,1024,2]{2,1,3,0:T(8,128)S(1)} %get-tuple-element.42, ...), kind=kOutput, calls=%fused_computation.34 | convolution fusion | flops 1099431936 | bytes 25788416 | tf_op jit(solution)/shard_map/qgmk,kgd->qgmd/dot_general | solution.py:54
  184.4 0.3 fusion.49
  184.9 20.2 %all_to_all.59 = bf16[8,128,512]{1,2,0:T(8,128)(2,1)S(1)} all-to-all(bf16[8,128,512]{1,2,0:T(8,128)(2,1)S(1)} %constant_dynamic-update-slice_fusion), channel_id=1, replica_groups=mesh['head'=8,'ctx'=32] {'head'}, dimensions={0} | all-to-all | bytes 2097152 | tf_op jit(solution)/shard_map/all_to_all | solution.py:16
  205.1 1.3 copy.74
  (18 shorter events, 0.2 us)
Async XLA Ops:
  2.0 14.8 %all-to-all-start = ((bf16[128,8,256]{0,2,1:T(8,128)(2,1)}), bf16[128,8,256]{0,2,1:T(8,128)(2,1)S(1)}, u32[]{:S(2)}, u32[]{:S(2)}) async-start(bf16[128,8,256]{0,2,1:T(8,128)(2,1)} %bitcast.1), calls=%async_computation | async-start | bytes 1048576 | tf_op jit(solution)/shard_map/all_to_all | solution.py:67
  16.8 13.7 %all-to-all-start.2 = ((bf16[128,8,256]{0,2,1:T(8,128)(2,1)}), bf16[128,8,256]{0,2,1:T(8,128)(2,1)S(1)}, u32[]{:S(2)}, u32[]{:S(2)}) async-start(bf16[128,8,256]{0,2,1:T(8,128)(2,1)} %bitcast.7), calls=%async_computation.2 | async-start | bytes 1048576 | tf_op jit(solution)/shard_map/all_to_all | solution.py:68
  30.6 25.6 %all-to-all-start.1 = ((bf16[128,8,512]{0,2,1:T(8,128)(2,1)}), bf16[128,8,512]{0,2,1:T(8,128)(2,1)}, u32[]{:S(2)}, u32[]{:S(2)}) async-start(bf16[128,8,512]{0,2,1:T(8,128)(2,1)} %bitcast.4), calls=%async_computation.1 | async-start | bytes 2097152 | tf_op jit(solution)/shard_map/all_to_all | solution.py:66
  35.7 36.5 %collective-permute-start.1 = (bf16[1024,512]{0,1:T(8,128)(2,1)}, bf16[1024,512]{0,1:T(8,128)(2,1)}, u32[]{:S(2)}, u32[]{:S(2)}) collective-permute-start(bf16[1024,512]{0,1:T(8,128)(2,1)} %bitcast_dynamic-update-slice_fusion), channel_id=1, source_target_pairs={{0,2},{1,3},{2,4},{3,5},{4,6},{5,7},{6,8},{7,9},{8,10},{9,11},{10,... | collective-permute-start | bytes 3145736 | tf_op jit(solution)/shard_map/ppermute | solution.py:29
  46.1 35.8 %collective-permute-start.2 = (bf16[1024,512]{0,1:T(8,128)(2,1)}, bf16[1024,512]{0,1:T(8,128)(2,1)}, u32[]{:S(2)}, u32[]{:S(2)}) collective-permute-start(bf16[1024,512]{0,1:T(8,128)(2,1)} %bitcast_dynamic-update-slice_fusion), channel_id=1, source_target_pairs={{0,3},{1,4},{2,5},{3,6},{4,7},{5,8},{6,9},{7,10},{8,11},{9,12},{10... | collective-permute-start | bytes 3145736 | tf_op jit(solution)/shard_map/ppermute | solution.py:29
  49.6 63.1 %collective-permute-start = (bf16[1024,512]{0,1:T(8,128)(2,1)}, bf16[1024,512]{0,1:T(8,128)(2,1)}, u32[]{:S(2)}, u32[]{:S(2)}) collective-permute-start(bf16[1024,512]{0,1:T(8,128)(2,1)} %bitcast_dynamic-update-slice_fusion), channel_id=1, source_target_pairs={{0,1},{1,2},{2,3},{3,4},{4,5},{5,6},{6,7},{7,8},{8,9},{9,10},{10,1... | collective-permute-start | bytes 3145736 | tf_op jit(solution)/shard_map/ppermute | solution.py:29
  61.4 12.9 %copy-start.2 = (bf16[1024,2,2,128]{0,3,2,1:T(8,128)(2,1)S(1)}, bf16[1024,2,2,128]{0,3,2,1:T(8,128)(2,1)}, u32[]{:S(2)}) copy-start(bf16[1024,2,2,128]{0,3,2,1:T(8,128)(2,1)} %reshape.353) | copy-start | bytes 3145732
  81.8 32.9 %copy-start = (pred[1024,1024]{0,1:T(8,128)(4,1)S(1)}, pred[1024,1024]{0,1:T(8,128)(4,1)}, u32[]{:S(2)}) copy-start(pred[1024,1024]{0,1:T(8,128)(4,1)} %get-tuple-element.36) | copy-start | bytes 3145732
  83.2 39.1 %copy-start.1 = (pred[1024,1024]{0,1:T(8,128)(4,1)S(1)}, pred[1024,1024]{0,1:T(8,128)(4,1)}, u32[]{:S(2)}) copy-start(pred[1024,1024]{0,1:T(8,128)(4,1)} %get-tuple-element.33) | copy-start | bytes 3145732
  132.6 13.7 %copy-start.4 = (bf16[1024,256]{0,1:T(8,128)(2,1)S(1)}, bf16[1024,256]{0,1:T(8,128)(2,1)}, u32[]{:S(2)}) copy-start(bf16[1024,256]{0,1:T(8,128)(2,1)} %get-tuple-element.22) | copy-start | bytes 1572868
  146.3 10.1 %copy-start.3 = (bf16[1024,256]{0,1:T(8,128)(2,1)S(1)}, bf16[1024,256]{0,1:T(8,128)(2,1)}, u32[]{:S(2)}) copy-start(bf16[1024,256]{0,1:T(8,128)(2,1)} %get-tuple-element.25) | copy-start | bytes 1572868
